TPU v7x, 128 devices: a whole 4x4x4 slice. The times are simulated.
128 devices in a mesh: req: 16 (over y, x), tp: 8 (over z, core).
Axes of the slice: x: 4, y: 4, z: 4, core: 2. Of those that a mesh axis runs over, the one named last changes fastest.
Arguments:
- stream: bfloat16 [512, 2048], P('req'), may hold values from -1.5 to 1.5
- attn_gain: bfloat16 [2048], replicated, may hold values from 0.25 to 1.75
- mlp_gain: bfloat16 [2048], replicated, may hold values from 0.25 to 1.75
- w_query: bfloat16 [2048, 2048], P(None, 'tp'), may hold values from -0.125 to 0.125
- w_keyval: bfloat16 [2048, 2, 2048], P(None, None, 'tp'), may hold values from -30 to 30
- w_out: bfloat16 [2048, 2048], P('tp'), may hold values from -0.125 to 0.125
- w_gate_up: bfloat16 [2048, 2, 8192], P(None, None, 'tp'), may hold values from -0.125 to 0.125
- w_down: bfloat16 [8192, 2048], P('tp'), may hold values from -0.0625 to 0.0625
- root_cache: bfloat16 [8, 4096, 2, 2048], P(None, 'req', None, 'tp'), may hold values from -240 to 240
- mid_cache: bfloat16 [16, 2048, 2, 2048], P('req', None, None, 'tp'), may hold values from -240 to 240
- leaf_cache: bfloat16 [512, 128, 2, 2048], P('req', None, None, 'tp'), may hold values from -240 to 240
- held_hidden: bfloat16 [16, 256, 2048], P('req', None, 'tp'), may hold values from -6 to 6
- recompute_rows: int32 [16, 256], P('req'), may hold values from 0 to 2047, as said below
- root_len: int32 [8], replicated, may hold values from 1024 to 4096
- mid_len: int32 [16], replicated, may hold values from 256 to 2048
- leaf_len: int32 [512], P('req'), may hold values from 1 to 128
- mid_parent: int32 [16], replicated, may hold values from 0 to 7
- leaf_parent: int32 [512], replicated, may hold values from 0 to 15
Outputs:
- layer_out: bfloat16 [512, 2048], P('req', 'tp')
Inputs may be any that keep to these rules, and one draw needn't show every extreme that they name: `recompute_rows`: the 256 slots of one middle node are distinct.
All inputs are finite; a program needn't handle non-finite values.
Results may differ from a plain program's by a relative error of at most 0.02.
The roundings to bfloat16 on the way count: a program that leaves them out, or rounds other values in their place, can miss the bound.
Values may be sent and summed in bfloat16 or wider, within the bound.
A program may use at most 192 MiB of HBM per device.

v0:
```python
import math
import jax
import jax.numpy as jnp
from jax import lax
from jax.sharding import PartitionSpec as P

D = 2048
HEAD_DIM = 64
EPSILON = 1e-05
THETA_BASE = 130000.0
NEG_FILL = -1e30


def combined_all(value, axis, combine):
    everything = jax.tree.map(lambda part: lax.all_gather(part, axis), value)
    first = jax.tree.map(lambda part: part[0], everything)

    def lap(k, so_far):
        return combine(so_far, jax.tree.map(lambda part: part[k], everything))

    return lax.fori_loop(1, lax.axis_size(axis), lap, first)


def rms_scale(values, gain):
    return (
        values
        * lax.rsqrt(jnp.mean(values * values, axis=-1, keepdims=True) + EPSILON)
        * gain.astype(jnp.float32)
    )


def rotate(values, positions):
    half_dim = values.shape[-1] // 2
    inv_freq = jnp.exp(
        jnp.arange(half_dim, dtype=jnp.float32) * (-2.0 * math.log(THETA_BASE) / values.shape[-1])
    )
    angles = positions.astype(jnp.float32)[..., None, None] * inv_freq
    cosines = jnp.cos(angles)
    sines = jnp.sin(angles)
    leading = values[..., :half_dim]
    trailing = values[..., half_dim:]
    return jnp.concatenate(
        [leading * cosines - trailing * sines, trailing * cosines + leading * sines], axis=-1
    )


def lookup(table_values, indices):
    hits = indices[..., None] == jnp.arange(table_values.shape[0], dtype=jnp.int32)
    return jnp.sum(jnp.where(hits, table_values, 0), axis=-1)


def partial_softmax(queries, key_rows, live_mask, score_scale):
    count = key_rows.shape[0]
    heads = queries.shape[1]
    key_part = key_rows[:, 0].reshape(count, heads, HEAD_DIM)
    value_part = key_rows[:, 1].reshape(count, heads, HEAD_DIM)
    scores = (
        jnp.einsum("bhd,khd->hbk", queries, key_part, preferred_element_type=jnp.float32)
        * score_scale
    )
    live = live_mask[None]
    row_max = jnp.max(jnp.where(live, scores, NEG_FILL), axis=2)
    weights = jnp.where(live, jnp.exp(scores - row_max[..., None]), 0.0)
    row_sum = jnp.sum(weights, axis=2)
    weighted = jnp.einsum(
        "hbk,khd->bhd", weights.astype(jnp.bfloat16), value_part, preferred_element_type=jnp.float32
    )
    return (row_max.T, row_sum.T, weighted.reshape(queries.shape[0], heads * HEAD_DIM))


def join(earlier, latter):
    best = jnp.maximum(earlier[0], latter[0])
    factor_one = jnp.exp(earlier[0] - best)
    factor_two = jnp.exp(latter[0] - best)
    row_sum = earlier[1] * factor_one + latter[1] * factor_two
    weighted = earlier[2] * jnp.repeat(factor_one, HEAD_DIM, axis=1) + latter[2] * jnp.repeat(
        factor_two, HEAD_DIM, axis=1
    )
    return (best, row_sum, weighted)


def leaf_softmax(queries, leaf_cache, leaf_len, score_scale):
    own_rows, slots = leaf_cache.shape[:2]
    heads = queries.shape[1]
    key_part = leaf_cache[:, :, 0].reshape(own_rows, slots, heads, HEAD_DIM)
    value_part = leaf_cache[:, :, 1].reshape(own_rows, slots, heads, HEAD_DIM)
    scores = (
        jnp.einsum("rhd,rkhd->rhk", queries, key_part, preferred_element_type=jnp.float32)
        * score_scale
    )
    live = (jnp.arange(slots, dtype=jnp.int32)[None, :] < leaf_len[:, None])[:, None, :]
    row_max = jnp.max(jnp.where(live, scores, NEG_FILL), axis=2)
    weights = jnp.where(live, jnp.exp(scores - row_max[..., None]), 0.0)
    row_sum = jnp.sum(weights, axis=2)
    weighted = jnp.einsum(
        "rhk,rkhd->rhd",
        weights.astype(jnp.bfloat16),
        value_part,
        preferred_element_type=jnp.float32,
    )
    return (row_max, row_sum, weighted)


def on_device(
    stream,
    attn_gain,
    mlp_gain,
    w_query,
    w_keyval,
    w_out,
    w_gate_up,
    w_down,
    root_cache,
    mid_cache,
    leaf_cache,
    held_hidden,
    recompute_rows,
    root_len,
    mid_len,
    leaf_len,
    mid_parent,
    leaf_parent,
):
    req_rank = lax.axis_index("req")
    own_rows = stream.shape[0]
    query_width = w_query.shape[1]
    local_heads = query_width // HEAD_DIM
    score_scale = HEAD_DIM ** (-0.5)
    requests = leaf_parent.shape[0]
    all_roots = lookup(mid_parent, leaf_parent)
    own_mids = lax.dynamic_slice_in_dim(leaf_parent, req_rank * own_rows, own_rows)
    own_roots = lax.dynamic_slice_in_dim(all_roots, req_rank * own_rows, own_rows)
    positions = lookup(root_len, own_roots) + lookup(mid_len, own_mids) + leaf_len
    stream_float = stream.astype(jnp.float32)
    normed = rms_scale(stream_float, attn_gain).astype(jnp.bfloat16)
    keyval_flat = w_keyval.reshape(D, 2 * query_width)
    queries = rotate(
        jnp.dot(normed, w_query, preferred_element_type=jnp.float32).reshape(
            own_rows, local_heads, HEAD_DIM
        ),
        positions,
    ).astype(jnp.bfloat16)
    fresh = jnp.dot(normed, keyval_flat, preferred_element_type=jnp.float32).reshape(
        own_rows, 2, local_heads, HEAD_DIM
    )
    key_new = rotate(fresh[:, 0], positions).astype(jnp.bfloat16)
    value_new = fresh[:, 1].astype(jnp.bfloat16)
    node_count, slots = mid_cache.shape[:2]
    recomp_count = recompute_rows.shape[1]
    held = lax.all_gather(held_hidden, "tp", axis=2, tiled=True)
    held_normed = rms_scale(held.astype(jnp.float32), attn_gain).astype(jnp.bfloat16)
    rebuilt = jnp.dot(
        held_normed.reshape(node_count * recomp_count, D),
        keyval_flat,
        preferred_element_type=jnp.float32,
    ).reshape(node_count, recomp_count, 2, local_heads, HEAD_DIM)
    own_nodes = req_rank * node_count + jnp.arange(node_count, dtype=jnp.int32)
    own_lens = lax.dynamic_slice_in_dim(mid_len, req_rank * node_count, node_count)
    own_parents = lax.dynamic_slice_in_dim(mid_parent, req_rank * node_count, node_count)
    rebuilt_pos = lookup(root_len, own_parents)[:, None] + recompute_rows
    rebuilt = (
        jnp.stack([rotate(rebuilt[:, :, 0], rebuilt_pos), rebuilt[:, :, 1]], axis=2)
        .astype(jnp.bfloat16)
        .reshape(node_count * recomp_count, 2, query_width)
    )
    all_queries = lax.all_gather(
        queries.reshape(own_rows, query_width), "req", axis=0, tiled=True
    ).reshape(requests, local_heads, HEAD_DIM)
    root_count, slice_len = root_cache.shape[:2]
    token_ids = req_rank * slice_len + jnp.arange(slice_len, dtype=jnp.int32)
    root_valid = token_ids[None, :] < root_len[:, None]
    root_match = all_roots[:, None] == jnp.arange(root_count, dtype=jnp.int32)[None, :]
    root_mask = (root_match[:, :, None] & root_valid[None]).reshape(
        requests, root_count * slice_len
    )
    root_part = partial_softmax(
        all_queries,
        root_cache.reshape(root_count * slice_len, 2, query_width),
        root_mask,
        score_scale,
    )
    replaced = jnp.any(
        recompute_rows[:, :, None] == jnp.arange(slots, dtype=jnp.int32)[None, None, :], axis=1
    )
    slot_live = (jnp.arange(slots, dtype=jnp.int32)[None, :] < own_lens[:, None]) & jnp.logical_not(
        replaced
    )
    belongs = leaf_parent[:, None] == own_nodes[None, :]
    held_mask = (belongs[:, :, None] & slot_live[None]).reshape(requests, node_count * slots)
    fresh_mask = (belongs[:, :, None] & (recompute_rows < own_lens[:, None])[None]).reshape(
        requests, node_count * recomp_count
    )
    mid_keys = jnp.concatenate(
        [mid_cache.reshape(node_count * slots, 2, query_width), rebuilt], axis=0
    )
    mid_part = partial_softmax(
        all_queries, mid_keys, jnp.concatenate([held_mask, fresh_mask], axis=1), score_scale
    )
    part_max, part_sum, part_acc = join(root_part, mid_part)
    merged_max, merged_sum, merged_acc = combined_all((part_max, part_sum, part_acc), "req", join)
    remote_max = lax.dynamic_slice_in_dim(merged_max, req_rank * own_rows, own_rows, 0)[None]
    remote_sum = lax.dynamic_slice_in_dim(merged_sum, req_rank * own_rows, own_rows, 0)[None]
    remote_acc = lax.dynamic_slice_in_dim(merged_acc, req_rank * own_rows, own_rows, 0)[None]
    leaf_max, leaf_sum, leaf_acc = leaf_softmax(queries, leaf_cache, leaf_len, score_scale)
    self_score = (
        jnp.sum(queries.astype(jnp.float32) * key_new.astype(jnp.float32), axis=-1) * score_scale
    )
    best = jnp.maximum(jnp.maximum(jnp.max(remote_max, axis=0), leaf_max), self_score)
    remote_factor = jnp.exp(remote_max - best[None])
    leaf_factor = jnp.exp(leaf_max - best)
    self_factor = jnp.exp(self_score - best)
    row_sum = jnp.sum(remote_sum * remote_factor, axis=0) + leaf_sum * leaf_factor + self_factor
    sources = remote_acc.shape[0]
    weighted = jnp.sum(
        remote_acc.reshape(sources, own_rows, local_heads, HEAD_DIM) * remote_factor[..., None],
        axis=0,
    )
    weighted = (
        weighted
        + leaf_acc * leaf_factor[..., None]
        + value_new.astype(jnp.float32) * self_factor[..., None]
    )
    attended = (weighted / row_sum[..., None]).reshape(own_rows, query_width).astype(jnp.bfloat16)
    attn_part = jnp.dot(attended, w_out, preferred_element_type=jnp.float32)
    width_share = D // lax.axis_size("tp")
    tp_rank = lax.axis_index("tp")
    residual = stream_float + lax.psum(attn_part, "tp")
    mixed_in = rms_scale(residual, mlp_gain).astype(jnp.bfloat16)
    residual_share = lax.dynamic_slice_in_dim(residual, tp_rank * width_share, width_share, 1)
    hidden_width = w_gate_up.shape[2]
    projected = jnp.dot(
        mixed_in, w_gate_up.reshape(D, 2 * hidden_width), preferred_element_type=jnp.float32
    ).reshape(own_rows, 2, hidden_width)
    hidden = (jax.nn.silu(projected[:, 0]) * projected[:, 1]).astype(jnp.bfloat16)
    down_share = lax.psum_scatter(
        jnp.dot(hidden, w_down, preferred_element_type=jnp.float32),
        "tp",
        scatter_dimension=1,
        tiled=True,
    )
    return (residual_share + down_share).astype(jnp.bfloat16)


def solution(mesh):
    placed = (
        P("req", None),
        P(),
        P(),
        P(None, "tp"),
        P(None, None, "tp"),
        P("tp", None),
        P(None, None, "tp"),
        P("tp", None),
        P(None, "req", None, "tp"),
        P("req", None, None, "tp"),
        P("req", None, None, "tp"),
        P("req", None, "tp"),
        P("req", None),
        P(),
        P(),
        P("req"),
        P(),
        P(),
    )
    return jax.shard_map(
        on_device, mesh=mesh, in_specs=placed, out_specs=P("req", "tp"), check_vma=False
    )
```

profile of v0, /device:TPU:0, one launch (start us, length us, event | category | flops | bytes accessed | tf_op | source)
XLA Modules:
  0.0 369.5 jit_solution(2306715656610677094)
XLA Ops:
  9.8 1.3 dynamic_slice.57
  11.1 1.2 dynamic_slice.56
  14.8 1.6 fusion.62
  16.6 2.1 copy.109
  18.7 2.5 copy.77
  21.2 2.8 fusion.44
  26.2 24.1 %all_gather.22 = bf16[512,256]{1,0:T(8,128)(2,1)S(1)} all-gather(bf16[32,256]{1,0:T(8,128)(2,1)S(1)} %convert_element_type.81), channel_id=1, replica_groups=mesh['req'=16,'tp'=8] {'req'}, dimensions={0}, use_global_device_ids=true | all-gather | bytes 278528 | tf_op jit(solution)/shard_map/all_gather | solution.py:166
  51.2 1.8 and.64
  53.0 1.6 copy.107
  54.6 4.2 %fusion.81 = (bf16[2048,1,256]{2,1,0:T(2,128)(2,1)}, bf16[2048,1,256]{2,1,0:T(2,128)(2,1)}) fusion(bf16[2048,2,256]{2,1,0:T(2,128)(2,1)S(1)} %bitcast.183), kind=kLoop, calls=%fused_computation.143 | loop fusion | bytes 4194304 | tf_op jit(solution)/shard_map/slice | solution.py:56
  58.8 6.0 %copy.103 = bf16[2048,1,256]{0,2,1:T(8,128)(2,1)} copy(bf16[2048,1,256]{2,1,0:T(2,128)(2,1)} %get-tuple-element.234) | data formatting | bytes 2097152
  64.8 1.3 fusion.70
  69.3 1.5 broadcast_and_fusion
  71.6 4.3 %copy.104 = bf16[2048,1,256]{0,2,1:T(8,128)(2,1)} copy(bf16[2048,1,256]{2,1,0:T(2,128)(2,1)S(1)} %copy-done.4) | data formatting | bytes 2097152
  75.9 1.9 broadcast_and_fusion.1
  77.9 2.5 pad_add_fusion
  80.3 4.5 %select_reduce_fusion.1 = (f32[4,512]{1,0:T(4,128)S(1)}, f32[4,512,2048]{2,1,0:T(8,128)S(1)}) fusion(pred[512,2048]{1,0:T(8,128)(4,1)S(1)} %broadcast_and_fusion.1, bf16[512,4,64]{0,2,1:T(8,128)(2,1)} %bitcast.189, bf16[2048,4,64]{0,2,1:T(8,128)(2,1)S(1)} %bitcast.188), kind=kOutput, calls=%fused_computation.13 | convolution fusion | flops 549451776 | bytes 19144704 | tf_op jit(solution)/shard_map/bhd,khd->hbk/dot_general | solution.py:58
  84.9 5.7 %copy-done.1 = f32[4,512,2048]{2,1,0:T(8,128)} copy-done((f32[4,512,2048]{2,1,0:T(8,128)}, f32[4,512,2048]{2,1,0:T(8,128)S(1)}, u32[]{:S(2)}) %copy-start.1) | copy-done | bytes 16777240
  90.6 5.2 %fusion.6 = f32[4,512]{1,0:T(4,128)} fusion(f32[4,512,2048]{2,1,0:T(8,128)S(1)} %get-tuple-element.253, f32[4,512]{1,0:T(4,128)S(1)} %get-tuple-element.252, pred[512,2048]{1,0:T(8,128)(4,1)S(1)} %broadcast_and_fusion.1), kind=kLoop, calls=%fused_computation.17 | loop fusion | flops 16775168 | bytes 17842176 | tf_op jit(solution)/shard_map/reduce_sum | solution.py:64
  95.8 1.5 fusion.13
  97.3 2.8 convolution_bitcast_fusion
  100.6 13.3 %maximum_maximum_fusion = bf16[2304,2,256]{2,1,0:T(2,128)(2,1)S(1)} fusion(bf16[256,1,256]{2,1,0:T(2,128)(2,1)S(1)} %copy.79, bf16[256,1,256]{2,1,0:T(2,128)(2,1)S(1)} %copy.78, bf16[2048,2,256]{2,1,0:T(2,128)(2,1)} %bitcast.196), kind=kLoop, calls=%fused_computation.25 | loop fusion | flops 7077888 | bytes 4718592 | tf_op jit(solution)/shard_map/concatenate | solution.py:193
  113.9 4.8 %fusion.80 = (bf16[2304,1,256]{2,1,0:T(2,128)(2,1)}, bf16[2304,1,256]{2,1,0:T(2,128)(2,1)}) fusion(bf16[2304,2,256]{2,1,0:T(2,128)(2,1)S(1)} %maximum_maximum_fusion), kind=kLoop, calls=%fused_computation.142 | loop fusion | bytes 4718592 | tf_op jit(solution)/shard_map/slice | solution.py:56
  118.7 6.0 %copy.80 = bf16[2304,1,256]{0,2,1:T(8,128)(2,1)} copy(bf16[2304,1,256]{2,1,0:T(2,128)(2,1)} %get-tuple-element.232) | data formatting | bytes 2359296 | tf_op jit(solution)/shard_map/slice | solution.py:55
  124.7 6.0 %copy.82 = bf16[2304,1,256]{0,2,1:T(8,128)(2,1)} copy(bf16[2304,1,256]{2,1,0:T(2,128)(2,1)} %get-tuple-element.231) | data formatting | bytes 2359296 | tf_op jit(solution)/shard_map/slice | solution.py:56
  130.7 5.6 %select_reduce_fusion = (f32[4,512]{1,0:T(4,128)S(1)}, f32[4,512,2304]{2,1,0:T(8,128)S(1)}) fusion(pred[512,2304]{1,0:T(8,128)(4,1)} %pad_add_fusion, bf16[512,4,64]{0,2,1:T(8,128)(2,1)} %bitcast.190, bf16[2304,4,64]{0,2,1:T(8,128)(2,1)} %bitcast.187), kind=kOutput, calls=%fused_computation.11 | convolution fusion | flops 618133504 | bytes 21504000 | tf_op jit(solution)/shard_map/bhd,khd->hbk/dot_general | solution.py:58
  136.4 5.1 %fusion.4 = f32[4,512]{1,0:T(4,128)S(1)} fusion(f32[4,512,2304]{2,1,0:T(8,128)S(1)} %get-tuple-element.251, f32[4,512]{1,0:T(4,128)S(1)} %get-tuple-element.250, pred[512,2304]{1,0:T(8,128)(4,1)S(1)} %copy-done.2), kind=kLoop, calls=%fused_computation.15 | loop fusion | flops 18872320 | bytes 20070400 | tf_op jit(solution)/shard_map/reduce_sum | solution.py:64
  142.1 6.8 %fusion.29 = f32[512,4,64]{0,2,1:T(8,128)} fusion(bf16[2304,4,64]{0,2,1:T(8,128)(2,1)} %bitcast.197, f32[4,512,2304]{2,1,0:T(8,128)S(1)} %get-tuple-element.251, f32[4,512]{1,0:T(4,128)S(1)} %get-tuple-element.250, pred[512,2304]{1,0:T(8,128)(4,1)} %pad_add_fusion, f32[512,4]{0,1:T(4,128)} %get-tuple-element.228), kind=kOutput, calls=%fused_computation.38 | convolution fusion | flops 622985216 | bytes 21774336 | tf_op jit(solution)/shard_map/hbk,khd->bhd/dot_general | solution.py:65
  148.9 8.0 %fusion.26 = f32[512,4,64]{0,2,1:T(8,128)S(1)} fusion(f32[512,4,64]{0,2,1:T(8,128)} %fusion.29, bf16[2048,4,64]{0,2,1:T(8,128)(2,1)} %bitcast.198, f32[4,512,2048]{2,1,0:T(8,128)} %copy-done.1, f32[4,512]{1,0:T(4,128)S(1)} %copy-done.14, pred[512,2048]{1,0:T(8,128)(4,1)S(1)} %broadcast_and_fusion.1, f32[512,4]{0,1:T(4,128)S(1)} %get-tuple-element.227), kind=kOutput, calls=%fused_computation.37 | convolution fusion | flops 553910272 | bytes 19939328 | tf_op jit(solution)/shard_map/hbk,khd->bhd/dot_general | solution.py:65
  158.0 10.0 %fusion.79 = (bf16[32,128,1,256]{3,2,1,0:T(2,128)(2,1)}, bf16[32,128,1,256]{3,2,1,0:T(2,128)(2,1)}) fusion(bf16[32,128,2,256]{3,2,1,0:T(2,128)(2,1)} %param.30), kind=kLoop, calls=%fused_computation.141 | loop fusion | bytes 8388608 | tf_op jit(solution)/shard_map/slice | solution.py:85
  168.0 9.8 %copy.105 = bf16[32,128,1,256]{1,3,0,2:T(8,128)(2,1)} copy(bf16[32,128,1,256]{3,2,1,0:T(2,128)(2,1)} %get-tuple-element.229) | data formatting | bytes 4194304
  177.8 8.6 %copy.106 = bf16[32,128,1,256]{1,3,0,2:T(8,128)(2,1)S(1)} copy(bf16[32,128,1,256]{3,2,1,0:T(2,128)(2,1)} %get-tuple-element.230) | data formatting | bytes 4194304
  186.5 2.2 fusion.56
  189.0 1.2 fusion.54
  190.2 23.4 %all-gather = f32[8192,4]{0,1:T(4,128)S(1)} all-gather(f32[512,4]{0,1:T(4,128)S(1)} %get-tuple-element.245), channel_id=2, replica_groups=mesh['req'=16,'tp'=8] {'req'}, dimensions={0}, use_global_device_ids=true | all-gather | bytes 139264 | tf_op jit(solution)/shard_map/all_gather | solution.py:15
  213.6 21.6 %all-gather.1 = f32[8192,4]{0,1:T(4,128)S(1)} all-gather(f32[512,4]{0,1:T(4,128)S(1)} %get-tuple-element.226), channel_id=3, replica_groups=mesh['req'=16,'tp'=8] {'req'}, dimensions={0}, use_global_device_ids=true | all-gather | bytes 139264 | tf_op jit(solution)/shard_map/all_gather | solution.py:15
  236.5 23.7 %while.19 = (s32[]{:T(128)}, f32[512,4]{0,1:T(4,128)S(1)}, f32[512,4]{0,1:T(4,128)S(1)}, f32[512,256]{0,1:T(8,128)S(1)}, f32[16,512,4]{1,2,0:T(4,128)S(1)}, /*in...) while((s32[]{:T(128)}, f32[512,4]{0,1:T(4,128)S(1)}, ...), condition=%wide.region_12.13_spmd, body=%wide.region_11.12_spmd.sunk | while | flops 405509 | bytes 3752087 | solution.py:21
  236.6 1.1 constant_dynamic-slice_fusion.3
  239.7 1.1 constant_dynamic-slice_fusion.3
  241.3 1.1 constant_dynamic-slice_fusion.3
  262.7 10.1 %copy.110 = bf16[256,8,2,1024]{3,1,2,0:T(8,128)(2,1)} copy(bf16[256,8,2,1024]{3,2,1,0:T(2,128)(2,1)} %bitcast.182) | data formatting | bytes 16777216
  272.8 12.4 %copy.91 = bf16[2048,2048]{1,0:T(8,128)(2,1)} copy(bf16[2048,2048]{0,1:T(8,128)(2,1)} %bitcast.181) | data formatting | bytes 16777216 | tf_op jit(solution)/shard_map/dot_general | solution.py:231
  285.2 37.8 %all-reduce.2.cloned.1.call-done = f32[32,2048]{1,0:T(8,128)} async-done(((f32[32,2048]{1,0:T(8,128)}), f32[32,2048]{1,0:T(8,128)}) %all-reduce.2.cloned.1.call-update) | async-done | bytes 262160 | tf_op jit(solution)/shard_map/psum | solution.py:227
  323.0 1.1 multiply_reduce_fusion
  324.1 6.1 %fusion.40 = f32[32,2,1024]{2,0,1:T(8,128)S(1)} fusion(bf16[2,1024,2048]{2,1,0:T(8,128)(2,1)} %bitcast.180, f32[32,2048]{1,0:T(8,128)S(1)} %get-tuple-element.219, f32[2048]{0:T(1024)S(1)} %convert_element_type.94, f32[32]{0:T(128)S(1)} %add_rsqrt_fusion.1), kind=kOutput, calls=%fused_computation.56 | convolution fusion | flops 268632064 | bytes 8921216 | tf_op jit(solution)/shard_map/dot_general | solution.py:231
  330.2 1.5 fusion.48
  331.8 29.8 %reduce-scatter.2.cloned.1.call-done = f32[32,256]{1,0:T(8,128)} async-done(((f32[32,2048]{1,0:T(8,128)}), f32[32,256]{1,0:T(8,128)}) %reduce-scatter.2.cloned.1.call-update) | async-done | bytes 32784 | tf_op jit(solution)/shard_map/reduce_scatter | solution.py:235
  361.6 1.4 add_convert_fusion.2
  (168 shorter events, 39.1 us)
Async XLA Ops:
  6.5 255.1 %copy-start = (bf16[256,2048]{1,0:T(8,128)(2,1)S(1)}, bf16[256,2048]{1,0:T(8,128)(2,1)}, u32[]{:S(2)}) copy-start(bf16[256,2048]{1,0:T(8,128)(2,1)} %param.25) | copy-start | bytes 3145732
  6.5 89.2 %all-gather.5.cloned.1.call-start = ((), (), s32[]{:S(2)}) async-start(), calls=%async_computation.1 | async-start | bytes 1179648 | tf_op jit(solution)/shard_map/all_gather | solution.py:150
  7.3 228.0 %all-gather.7.cloned.1.call-start = ((), (), s32[]{:S(2)}) async-start(), calls=%async_computation.2 | async-start | bytes 8912896 | tf_op jit(solution)/shard_map/all_gather | solution.py:15
  16.6 4.6 %copy-start.7 = (bf16[32,2048]{1,0:T(8,128)(2,1)S(1)}, bf16[32,2048]{1,0:T(8,128)(2,1)}, u32[]{:S(2)}) copy-start(bf16[32,2048]{1,0:T(8,128)(2,1)} %param.20) | copy-start | bytes 393220
  18.7 5.4 %copy-start.21 = (s32[8]{0:T(128)S(1)}, s32[8]{0:T(128)}, u32[]{:S(2)}) copy-start(s32[8]{0:T(128)} %param.33) | copy-start | bytes 100
  18.7 5.5 %copy-start.19 = (s32[32]{0:T(128)S(1)}, s32[32]{0:T(128)}, u32[]{:S(2)}) copy-start(s32[32]{0:T(128)} %param.35) | copy-start | bytes 388
  21.2 33.4 %copy-start.3 = (bf16[8,256,2,256]{3,2,1,0:T(2,128)(2,1)S(1)}, bf16[8,256,2,256]{3,2,1,0:T(2,128)(2,1)}, u32[]{:S(2)}) copy-start(bf16[8,256,2,256]{3,2,1,0:T(2,128)(2,1)} %param.28) | copy-start | bytes 6291460
  24.1 0.7 copy-start.9
  25.5 0.6 copy-start.11
  54.6 11.5 %copy-start.18 = (s32[1,256]{1,0:T(1,128)S(1)}, s32[1,256]{1,0:T(1,128)}, u32[]{:S(2)}) copy-start(s32[1,256]{1,0:T(1,128)} %param.32) | copy-start | bytes 3076
  58.8 12.8 %copy-start.4 = (bf16[2048,1,256]{2,1,0:T(2,128)(2,1)S(1)}, bf16[2048,1,256]{2,1,0:T(2,128)(2,1)}, u32[]{:S(2)}) copy-start(bf16[2048,1,256]{2,1,0:T(2,128)(2,1)} %get-tuple-element.233) | copy-start | bytes 3145732
  75.9 4.5 %copy-start.5 = (bf16[2048,1,256]{0,2,1:T(8,128)(2,1)S(1)}, bf16[2048,1,256]{0,2,1:T(8,128)(2,1)}, u32[]{:S(2)}) copy-start(bf16[2048,1,256]{0,2,1:T(8,128)(2,1)} %copy.103) | copy-start | bytes 3145732
  84.9 5.7 %copy-start.1 = (f32[4,512,2048]{2,1,0:T(8,128)}, f32[4,512,2048]{2,1,0:T(8,128)S(1)}, u32[]{:S(2)}) copy-start(f32[4,512,2048]{2,1,0:T(8,128)S(1)} %get-tuple-element.253) | copy-start | bytes 50331652
  84.9 5.7 %copy-start.13 = (f32[4,512]{1,0:T(4,128)}, f32[4,512]{1,0:T(4,128)S(1)}, u32[]{:S(2)}) copy-start(f32[4,512]{1,0:T(4,128)S(1)} %get-tuple-element.252) | copy-start | bytes 24580
  95.8 4.3 %copy-start.10 = (f32[256,32]{0,1:T(8,128)S(1)}, f32[256,32]{0,1:T(8,128)}, u32[]{:S(2)}) copy-start(f32[256,32]{0,1:T(8,128)} %get-tuple-element.247) | copy-start | bytes 98308
  130.7 5.6 %copy-start.2 = (pred[512,2304]{1,0:T(8,128)(4,1)S(1)}, pred[512,2304]{1,0:T(8,128)(4,1)}, u32[]{:S(2)}) copy-start(pred[512,2304]{1,0:T(8,128)(4,1)} %pad_add_fusion) | copy-start | bytes 3538948
  136.4 5.1 %copy-start.14 = (f32[4,512]{1,0:T(4,128)S(1)}, f32[4,512]{1,0:T(4,128)}, u32[]{:S(2)}) copy-start(f32[4,512]{1,0:T(4,128)} %copy-done.13) | copy-start | bytes 24580
  136.4 5.1 %copy-start.15 = (f32[4,512]{1,0:T(4,128)S(1)}, f32[4,512]{1,0:T(4,128)}, u32[]{:S(2)}) copy-start(f32[4,512]{1,0:T(4,128)} %fusion.6) | copy-start | bytes 24580
  157.9 165.1 %all-reduce.2.cloned.1.call-start = ((), (), s32[]{:S(2)}) async-start(), calls=%async_computation.3 | async-start | bytes 524288 | tf_op jit(solution)/shard_map/psum | solution.py:227
  177.8 8.6 %copy-start.20 = (s32[32]{0:T(128)S(1)}, s32[32]{0:T(128)}, u32[]{:S(2)}) copy-start(s32[32]{0:T(128)} %param.35) | copy-start | bytes 388
  177.8 8.7 %copy-start.12 = (bf16[32,4,64]{2,0,1:T(8,128)(2,1)S(1)}, bf16[32,4,64]{2,0,1:T(8,128)(2,1)}, u32[]{:S(2)}) copy-start(bf16[32,4,64]{2,0,1:T(8,128)(2,1)} %copy-done.11) | copy-start | bytes 49156
  236.5 23.9 %copy-start.16 = (f32[32,4]{0,1:T(4,128)S(1)}, f32[32,4]{0,1:T(4,128)}, u32[]{:S(2)}) copy-start(f32[32,4]{0,1:T(4,128)} %get-tuple-element.224) | copy-start | bytes 1540
  262.6 99.0 %reduce-scatter.2.cloned.1.call-start = ((), (), s32[]{:S(2)}) async-start(), calls=%async_computation.4 | async-start | bytes 294912 | tf_op jit(solution)/shard_map/reduce_scatter | solution.py:235
  272.8 12.4 %copy-start.17 = (bf16[2048]{0:T(1024)(128)(2,1)S(1)}, bf16[2048]{0:T(1024)(128)(2,1)}, u32[]{:S(2)}) copy-start(bf16[2048]{0:T(1024)(128)(2,1)} %param.22) | copy-start | bytes 12292
  272.8 50.2 %copy-start.8 = (bf16[32,2048]{1,0:T(8,128)(2,1)S(1)}, bf16[32,2048]{1,0:T(8,128)(2,1)}, u32[]{:S(2)}) copy-start(bf16[32,2048]{1,0:T(8,128)(2,1)} %param.20) | copy-start | bytes 393220
  324.1 6.2 %copy-start.6 = (bf16[1024,2048]{1,0:T(8,128)(2,1)S(1)}, bf16[1024,2048]{1,0:T(8,128)(2,1)}, u32[]{:S(2)}) copy-start(bf16[1024,2048]{1,0:T(8,128)(2,1)} %param.27) | copy-start | bytes 12582916
Sparse Core Ops, SparseCore 0:
  9.0 26.0 all-gather.4
  158.0 71.9 all-gather.6
  262.7 60.1 all-reduce.1
  331.9 29.6 reduce-scatter.1
where the time goes:
time: 372 us; the launch traced here: 370 us
  local copies, waits for them, and re-layouts  124 us (33%)
  blocking collectives  69.1 us (19%)
  waiting for transfers between devices  68.4 us (18%)
  other arithmetic  50 us (13%)
  matrix products  44.2 us (12%)
  between operations  13.5 us (4%)
    unnamed x53, local copies, waits for them, and re-layouts  49.1 us
    all_gather x2, blocking collectives, combined_all(): everything = jax.tree.map(lambda part: lax.all_gather(part, axis), value)  45 us
    psum x1, waiting for transfers between devices, on_device(): residual = stream_float + lax.psum(attn_part, 'tp')  37.8 us
    reduce_scatter x1, waiting for transfers between devices, on_device(): lax.psum_scatter(jnp.dot(hidden, w_down, preferred_element_type=jnp.float...  29.8 us
    all_gather x1, blocking collectives, on_device(): lax.all_gather(queries.reshape(own_rows, query_width), 'req', axis=0, til...  24.1 us
    dynamic_slice x30, local copies, waits for them, and re-layouts, lap(): return combine(so_far, jax.tree.map(lambda part: part[k], everything))  19.2 us
    slice x3, local copies, waits for them, and re-layouts, partial_softmax(): value_part = key_rows[:, 1].reshape(count, heads, HEAD_DIM)  15 us
    dot_general x2, matrix products, partial_softmax(): jnp.einsum('hbk,khd->bhd', weights.astype(jnp.bfloat16), value_part, pref...  14.8 us
  transfers between devices with their start and end apart: 4, of which 2 were waited for; matrix products, arithmetic and copies ran while one was open for 30% of the time, Pallas kernels for 0%

commit v1 on v0

--- a/solution.py
+++ b/solution.py
@@ -9,6 +9,11 @@
 EPSILON = 1e-05
 THETA_BASE = 130000.0
 NEG_FILL = -1e30
+
+
+def gather_over(x, name, dim):
+    sent = jnp.stack([x] * lax.axis_size(name))
+    return jnp.concatenate(lax.all_to_all(sent, name, 0, 0), axis=dim)
 
 
 def combined_all(value, axis, combine):
@@ -163,9 +168,9 @@
         .astype(jnp.bfloat16)
         .reshape(node_count * recomp_count, 2, query_width)
     )
-    all_queries = lax.all_gather(
-        queries.reshape(own_rows, query_width), "req", axis=0, tiled=True
-    ).reshape(requests, local_heads, HEAD_DIM)
+    all_queries = gather_over(queries.reshape(own_rows, query_width), "req", 0).reshape(
+        requests, local_heads, HEAD_DIM
+    )
     root_count, slice_len = root_cache.shape[:2]
     token_ids = req_rank * slice_len + jnp.arange(slice_len, dtype=jnp.int32)
     root_valid = token_ids[None, :] < root_len[:, None]

time: 372 us -> 354 us (0.952)
  blocking collectives: 69.1 us -> 47.3 us
  starting transfers between devices: 0.13 us -> 7.62 us
  other arithmetic: 50 us -> 44.5 us
    all_gather x1 -> x0, blocking collectives: 24.1 us -> none  [on_device(): lax.all_gather(queries.reshape(own_rows, query_width), 'req', axis=0, til...]
    all_to_all x0 -> x1, starting transfers between devices: none -> 7.17 us  [gather_over(): return jnp.concatenate(lax.all_to_all(sent, name, 0, 0), axis=dim)]
    another operation x0 -> x3, local copies, waits for them, and re-layouts: none -> 4.08 us  [the longest x2 3.33 us: on_device(): gather_over(queries.reshape(own_rows, query_width), 'req', 0)]
    unnamed x53 -> x59, local copies, waits for them, and re-layouts: 49.1 us -> 47.7 us
  transfers between devices with their start and end apart: 4 -> 5, of which waited for: 2 -> 2; matrix products, arithmetic and copies ran while one was open for 30% -> 26% of each run, Pallas kernels for 0% -> 0%
where the time goes in v1:
time: 354 us; the launch traced here: 349 us
  local copies, waits for them, and re-layouts  124 us (35%)
  waiting for transfers between devices  67.6 us (19%)
  blocking collectives  47.3 us (13%)
  other arithmetic  44.5 us (13%)
  matrix products  43.1 us (12%)
  between operations  13.9 us (4%)
  starting transfers between devices  7.62 us (2%)
    unnamed x59, local copies, waits for them, and re-layouts  47.7 us
    all_gather x2, blocking collectives, combined_all(): everything = jax.tree.map(lambda part: lax.all_gather(part, axis), value)  47.3 us
    psum x1, waiting for transfers between devices, on_device(): residual = stream_float + lax.psum(attn_part, 'tp')  37 us
    reduce_scatter x1, waiting for transfers between devices, on_device(): lax.psum_scatter(jnp.dot(hidden, w_down, preferred_element_type=jnp.float...  29.8 us
    dynamic_slice x30, local copies, waits for them, and re-layouts, lap(): return combine(so_far, jax.tree.map(lambda part: part[k], everything))  19.2 us
    slice x3, local copies, waits for them, and re-layouts, partial_softmax(): value_part = key_rows[:, 1].reshape(count, heads, HEAD_DIM)  15.1 us
    dot_general x2, matrix products, partial_softmax(): jnp.einsum('hbk,khd->bhd', weights.astype(jnp.bfloat16), value_part, pref...  15 us
    concatenate x1, other arithmetic, on_device(): jnp.concatenate([mid_cache.reshape(node_count * slots, 2, query_width), r...  13.8 us
  transfers between devices with their start and end apart: 5, of which 2 were waited for; matrix products, arithmetic and copies ran while one was open for 26% of the time, Pallas kernels for 0%

profile of v1, /device:TPU:0, one launch (start us, length us, event | category | flops | bytes accessed | tf_op | source)
XLA Modules:
  0.0 348.6 jit_solution(2424717255625928734)
XLA Ops:
  10.0 1.6 fusion.62
  11.8 2.1 copy.112
  14.0 2.4 copy.79
  16.4 2.8 fusion.44
  21.6 7.2 %all-to-all-start = ((bf16[16,32,256]{2,1,0:T(8,128)(2,1)}), bf16[16,32,256]{2,1,0:T(8,128)(2,1)}, u32[]{:S(2)}, u32[]{:S(2)}) async-start(bf16[16,32,256]{2,1,0:T(8,128)(2,1)} %stack.11), calls=%async_computation | async-start | bytes 524288 | tf_op jit(solution)/shard_map/all_to_all | solution.py:16
  31.2 1.6 and.64
  33.5 4.2 %fusion.81 = (bf16[2048,1,256]{2,1,0:T(2,128)(2,1)}, bf16[2048,1,256]{2,1,0:T(2,128)(2,1)}) fusion(bf16[2048,2,256]{2,1,0:T(2,128)(2,1)S(1)} %bitcast.182), kind=kLoop, calls=%fused_computation.143 | loop fusion | bytes 4194304 | tf_op jit(solution)/shard_map/slice | solution.py:61
  37.7 1.3 fusion.70
  42.1 1.1 pad_add_fusion
  44.0 4.6 %copy.106 = bf16[2048,1,256]{0,2,1:T(8,128)(2,1)S(1)} copy(bf16[2048,1,256]{2,1,0:T(2,128)(2,1)} %get-tuple-element.234) | data formatting | bytes 2097152
  48.5 5.9 %copy.107 = bf16[2048,1,256]{0,2,1:T(8,128)(2,1)} copy(bf16[2048,1,256]{2,1,0:T(2,128)(2,1)} %get-tuple-element.233) | data formatting | bytes 2097152
  54.6 2.0 reshape_reshape.3
  56.6 1.3 copy.78
  57.9 3.3 select_reduce_fusion.1
  61.2 5.7 %copy-done.1 = f32[4,512,2048]{2,1,0:T(8,128)} copy-done((f32[4,512,2048]{2,1,0:T(8,128)}, f32[4,512,2048]{2,1,0:T(8,128)S(1)}, u32[]{:S(2)}) %copy-start.1) | copy-done | bytes 16777240
  66.9 5.2 %fusion.6 = f32[4,512]{1,0:T(4,128)} fusion(f32[4,512,2048]{2,1,0:T(8,128)S(1)} %get-tuple-element.253, f32[4,512]{1,0:T(4,128)S(1)} %get-tuple-element.252, pred[512,2048]{1,0:T(8,128)(4,1)S(1)} %broadcast_and_fusion.1), kind=kLoop, calls=%fused_computation.17 | loop fusion | flops 16775168 | bytes 17842176 | tf_op jit(solution)/shard_map/reduce_sum | solution.py:69
  72.1 1.5 fusion.13
  73.7 2.7 convolution_bitcast_fusion
  76.9 13.8 %maximum_maximum_fusion = bf16[2304,2,256]{2,1,0:T(2,128)(2,1)S(1)} fusion(bf16[256,1,256]{2,1,0:T(2,128)(2,1)S(1)} %copy.81, bf16[256,1,256]{2,1,0:T(2,128)(2,1)S(1)} %copy.80, bf16[2048,2,256]{2,1,0:T(2,128)(2,1)} %bitcast.193), kind=kLoop, calls=%fused_computation.25 | loop fusion | flops 7077888 | bytes 4718592 | tf_op jit(solution)/shard_map/concatenate | solution.py:198
  90.7 4.8 %fusion.80 = (bf16[2304,1,256]{2,1,0:T(2,128)(2,1)}, bf16[2304,1,256]{2,1,0:T(2,128)(2,1)}) fusion(bf16[2304,2,256]{2,1,0:T(2,128)(2,1)S(1)} %maximum_maximum_fusion), kind=kLoop, calls=%fused_computation.142 | loop fusion | bytes 4718592 | tf_op jit(solution)/shard_map/slice | solution.py:61
  95.5 6.0 %copy.82 = bf16[2304,1,256]{0,2,1:T(8,128)(2,1)} copy(bf16[2304,1,256]{2,1,0:T(2,128)(2,1)} %get-tuple-element.232) | data formatting | bytes 2359296 | tf_op jit(solution)/shard_map/slice | solution.py:60
  101.6 6.1 %copy.85 = bf16[2304,1,256]{0,2,1:T(8,128)(2,1)} copy(bf16[2304,1,256]{2,1,0:T(2,128)(2,1)} %get-tuple-element.231) | data formatting | bytes 2359296 | tf_op jit(solution)/shard_map/slice | solution.py:61
  107.6 5.6 %select_reduce_fusion = (f32[4,512]{1,0:T(4,128)S(1)}, f32[4,512,2304]{2,1,0:T(8,128)S(1)}) fusion(pred[512,2304]{1,0:T(8,128)(4,1)} %pad_add_fusion, bf16[512,4,64]{0,2,1:T(8,128)(2,1)} %copy-done.4, bf16[2304,4,64]{0,2,1:T(8,128)(2,1)} %bitcast.186), kind=kOutput, calls=%fused_computation.11 | convolution fusion | flops 618133504 | bytes 21504000 | tf_op jit(solution)/shard_map/bhd,khd->hbk/dot_general | solution.py:63
  113.3 5.1 %fusion.4 = f32[4,512]{1,0:T(4,128)S(1)} fusion(f32[4,512,2304]{2,1,0:T(8,128)S(1)} %get-tuple-element.251, f32[4,512]{1,0:T(4,128)S(1)} %get-tuple-element.250, pred[512,2304]{1,0:T(8,128)(4,1)S(1)} %copy-done.2), kind=kLoop, calls=%fused_computation.15 | loop fusion | flops 18872320 | bytes 20070400 | tf_op jit(solution)/shard_map/reduce_sum | solution.py:69
  119.0 6.8 %fusion.29 = f32[512,4,64]{0,2,1:T(8,128)} fusion(bf16[2304,4,64]{0,2,1:T(8,128)(2,1)} %bitcast.194, f32[4,512,2304]{2,1,0:T(8,128)S(1)} %get-tuple-element.251, f32[4,512]{1,0:T(4,128)S(1)} %get-tuple-element.250, pred[512,2304]{1,0:T(8,128)(4,1)} %pad_add_fusion, f32[512,4]{0,1:T(4,128)} %get-tuple-element.228), kind=kOutput, calls=%fused_computation.38 | convolution fusion | flops 622985216 | bytes 21774336 | tf_op jit(solution)/shard_map/hbk,khd->bhd/dot_general | solution.py:70
  125.8 8.2 %fusion.26 = f32[512,4,64]{0,2,1:T(8,128)S(1)} fusion(f32[512,4,64]{0,2,1:T(8,128)} %fusion.29, bf16[2048,4,64]{0,2,1:T(8,128)(2,1)} %bitcast.195, f32[4,512,2048]{2,1,0:T(8,128)} %copy-done.1, f32[4,512]{1,0:T(4,128)} %copy-done.9, pred[512,2048]{1,0:T(8,128)(4,1)S(1)} %broadcast_and_fusion.1, f32[512,4]{0,1:T(4,128)} %get-tuple-element.227), kind=kOutput, calls=%fused_computation.37 | convolution fusion | flops 553910272 | bytes 19939328 | tf_op jit(solution)/shard_map/hbk,khd->bhd/dot_general | solution.py:70
  135.1 10.0 %fusion.79 = (bf16[32,128,1,256]{3,2,1,0:T(2,128)(2,1)}, bf16[32,128,1,256]{3,2,1,0:T(2,128)(2,1)}) fusion(bf16[32,128,2,256]{3,2,1,0:T(2,128)(2,1)} %param.30), kind=kLoop, calls=%fused_computation.141 | loop fusion | bytes 8388608 | tf_op jit(solution)/shard_map/slice | solution.py:90
  145.1 9.7 %copy.108 = bf16[32,128,1,256]{1,3,0,2:T(8,128)(2,1)} copy(bf16[32,128,1,256]{3,2,1,0:T(2,128)(2,1)} %get-tuple-element.229) | data formatting | bytes 4194304
  154.9 8.7 %copy.109 = bf16[32,128,1,256]{1,3,0,2:T(8,128)(2,1)S(1)} copy(bf16[32,128,1,256]{3,2,1,0:T(2,128)(2,1)} %get-tuple-element.230) | data formatting | bytes 4194304
  163.6 2.2 fusion.56
  166.1 1.2 fusion.54
  167.3 24.2 %all-gather = f32[8192,4]{0,1:T(4,128)S(1)} all-gather(f32[512,4]{0,1:T(4,128)S(1)} %copy-done.13), channel_id=2, replica_groups=mesh['req'=16,'tp'=8] {'req'}, dimensions={0}, use_global_device_ids=true | all-gather | bytes 139264 | tf_op jit(solution)/shard_map/all_gather | solution.py:20
  191.5 23.1 %all-gather.1 = f32[8192,4]{0,1:T(4,128)S(1)} all-gather(f32[512,4]{0,1:T(4,128)S(1)} %copy-done.12), channel_id=3, replica_groups=mesh['req'=16,'tp'=8] {'req'}, dimensions={0}, use_global_device_ids=true | all-gather | bytes 139264 | tf_op jit(solution)/shard_map/all_gather | solution.py:20
  216.0 23.7 %while.19 = (s32[]{:T(128)}, f32[512,4]{0,1:T(4,128)S(1)}, f32[512,4]{0,1:T(4,128)S(1)}, f32[512,256]{0,1:T(8,128)S(1)}, f32[16,512,4]{1,2,0:T(4,128)S(1)}, /*in...) while((s32[]{:T(128)}, f32[512,4]{0,1:T(4,128)S(1)}, ...), condition=%wide.region_12.13_spmd, body=%wide.region_11.12_spmd.sunk | while | flops 405509 | bytes 3752087 | solution.py:26
  216.0 1.1 constant_dynamic-slice_fusion.3
  217.6 1.1 constant_dynamic-slice_fusion.3
  219.2 1.1 constant_dynamic-slice_fusion.3
  220.8 1.1 constant_dynamic-slice_fusion.3
  222.3 1.1 constant_dynamic-slice_fusion.3
  223.9 1.1 constant_dynamic-slice_fusion.3
  242.1 10.1 %copy.113 = bf16[256,8,2,1024]{3,1,2,0:T(8,128)(2,1)} copy(bf16[256,8,2,1024]{3,2,1,0:T(2,128)(2,1)} %bitcast.181) | data formatting | bytes 16777216
  252.3 12.5 %copy.94 = bf16[2048,2048]{1,0:T(8,128)(2,1)} copy(bf16[2048,2048]{0,1:T(8,128)(2,1)} %bitcast.180) | data formatting | bytes 16777216 | tf_op jit(solution)/shard_map/dot_general | solution.py:236
  264.8 37.0 %all-reduce.2.cloned.1.call-done = f32[32,2048]{1,0:T(8,128)} async-done(((f32[32,2048]{1,0:T(8,128)}), f32[32,2048]{1,0:T(8,128)}) %all-reduce.2.cloned.1.call-update) | async-done | bytes 262160 | tf_op jit(solution)/shard_map/psum | solution.py:232
  301.8 1.1 multiply_reduce_fusion
  302.9 6.1 %fusion.40 = f32[32,2,1024]{2,0,1:T(8,128)S(1)} fusion(bf16[2,1024,2048]{2,1,0:T(8,128)(2,1)} %bitcast.179, f32[32,2048]{1,0:T(8,128)S(1)} %get-tuple-element.219, f32[2048]{0:T(1024)S(1)} %convert_element_type.95, f32[32]{0:T(128)S(1)} %add_rsqrt_fusion.1), kind=kOutput, calls=%fused_computation.56 | convolution fusion | flops 268632064 | bytes 8921216 | tf_op jit(solution)/shard_map/dot_general | solution.py:236
  309.1 1.5 fusion.48
  310.6 29.8 %reduce-scatter.2.cloned.1.call-done = f32[32,256]{1,0:T(8,128)} async-done(((f32[32,2048]{1,0:T(8,128)}), f32[32,256]{1,0:T(8,128)}) %reduce-scatter.2.cloned.1.call-update) | async-done | bytes 32784 | tf_op jit(solution)/shard_map/reduce_scatter | solution.py:240
  340.5 1.4 add_convert_fusion.2
  (177 shorter events, 35.9 us)
Async XLA Ops:
  6.5 234.6 %copy-start = (bf16[256,2048]{1,0:T(8,128)(2,1)S(1)}, bf16[256,2048]{1,0:T(8,128)(2,1)}, u32[]{:S(2)}) copy-start(bf16[256,2048]{1,0:T(8,128)(2,1)} %param.25) | copy-start | bytes 3145732
  6.5 12.9 %copy-start.18 = (f32[32]{0:T(128)}, f32[32]{0:T(128)S(1)}, u32[]{:S(2)}) copy-start(f32[32]{0:T(128)S(1)} %multiply_exponential_fusion) | copy-start | bytes 388
  11.8 4.6 %copy-start.6 = (bf16[32,2048]{1,0:T(8,128)(2,1)S(1)}, bf16[32,2048]{1,0:T(8,128)(2,1)}, u32[]{:S(2)}) copy-start(bf16[32,2048]{1,0:T(8,128)(2,1)} %param.20) | copy-start | bytes 393220
  13.9 5.4 %copy-start.23 = (s32[8]{0:T(128)S(1)}, s32[8]{0:T(128)}, u32[]{:S(2)}) copy-start(s32[8]{0:T(128)} %param.33) | copy-start | bytes 100
  13.9 5.5 %copy-start.24 = (s32[16]{0:T(128)S(1)}, s32[16]{0:T(128)}, u32[]{:S(2)}) copy-start(s32[16]{0:T(128)} %param.34) | copy-start | bytes 196
  13.9 5.5 %copy-start.20 = (s32[32]{0:T(128)S(1)}, s32[32]{0:T(128)}, u32[]{:S(2)}) copy-start(s32[32]{0:T(128)} %param.35) | copy-start | bytes 388
  14.0 16.0 %copy-start.22 = (s32[16]{0:T(128)S(1)}, s32[16]{0:T(128)}, u32[]{:S(2)}) copy-start(s32[16]{0:T(128)} %param.36) | copy-start | bytes 196
  14.0 17.2 %copy-start.14 = (s32[512]{0:T(512)S(1)}, s32[512]{0:T(512)}, u32[]{:S(2)}) copy-start(s32[512]{0:T(512)} %param.37) | copy-start | bytes 6148
  16.4 17.0 %copy-start.3 = (bf16[8,256,2,256]{3,2,1,0:T(2,128)(2,1)S(1)}, bf16[8,256,2,256]{3,2,1,0:T(2,128)(2,1)}, u32[]{:S(2)}) copy-start(bf16[8,256,2,256]{3,2,1,0:T(2,128)(2,1)} %param.28) | copy-start | bytes 6291460
  19.3 0.7 copy-start.8
  21.6 33.0 %all-to-all-start = ((bf16[16,32,256]{2,1,0:T(8,128)(2,1)}), bf16[16,32,256]{2,1,0:T(8,128)(2,1)}, u32[]{:S(2)}, u32[]{:S(2)}) async-start(bf16[16,32,256]{2,1,0:T(8,128)(2,1)} %stack.11), calls=%async_computation | async-start | bytes 524288 | tf_op jit(solution)/shard_map/all_to_all | solution.py:16
  28.8 43.4 %all-gather.5.cloned.1.call-start = ((), (), s32[]{:S(2)}) async-start(), calls=%async_computation.2 | async-start | bytes 1179648 | tf_op jit(solution)/shard_map/all_gather | solution.py:155
  29.5 185.2 %all-gather.7.cloned.1.call-start = ((), (), s32[]{:S(2)}) async-start(), calls=%async_computation.3 | async-start | bytes 8912896 | tf_op jit(solution)/shard_map/all_gather | solution.py:20
  33.5 5.5 %copy-start.17 = (s32[1,256]{1,0:T(1,128)S(1)}, s32[1,256]{1,0:T(1,128)}, u32[]{:S(2)}) copy-start(s32[1,256]{1,0:T(1,128)} %param.32) | copy-start | bytes 3076
  42.1 12.3 %copy-start.19 = (f32[32]{0:T(128)S(1)}, f32[32]{0:T(128)}, u32[]{:S(2)}) copy-start(f32[32]{0:T(128)} %copy-done.18) | copy-start | bytes 388
  57.9 3.3 copy-start.4
  61.2 5.7 %copy-start.1 = (f32[4,512,2048]{2,1,0:T(8,128)}, f32[4,512,2048]{2,1,0:T(8,128)S(1)}, u32[]{:S(2)}) copy-start(f32[4,512,2048]{2,1,0:T(8,128)S(1)} %get-tuple-element.253) | copy-start | bytes 50331652
  61.2 10.9 %copy-start.9 = (f32[4,512]{1,0:T(4,128)}, f32[4,512]{1,0:T(4,128)S(1)}, u32[]{:S(2)}) copy-start(f32[4,512]{1,0:T(4,128)S(1)} %get-tuple-element.252) | copy-start | bytes 24580
  107.6 5.6 %copy-start.2 = (pred[512,2304]{1,0:T(8,128)(4,1)S(1)}, pred[512,2304]{1,0:T(8,128)(4,1)}, u32[]{:S(2)}) copy-start(pred[512,2304]{1,0:T(8,128)(4,1)} %pad_add_fusion) | copy-start | bytes 3538948
  113.3 5.1 %copy-start.10 = (f32[4,512]{1,0:T(4,128)S(1)}, f32[4,512]{1,0:T(4,128)}, u32[]{:S(2)}) copy-start(f32[4,512]{1,0:T(4,128)} %copy-done.9) | copy-start | bytes 24580
  113.3 5.1 %copy-start.11 = (f32[4,512]{1,0:T(4,128)S(1)}, f32[4,512]{1,0:T(4,128)}, u32[]{:S(2)}) copy-start(f32[4,512]{1,0:T(4,128)} %fusion.6) | copy-start | bytes 24580
  135.0 166.8 %all-reduce.2.cloned.1.call-start = ((), (), s32[]{:S(2)}) async-start(), calls=%async_computation.4 | async-start | bytes 524288 | tf_op jit(solution)/shard_map/psum | solution.py:232
  154.8 8.7 %copy-start.21 = (s32[32]{0:T(128)S(1)}, s32[32]{0:T(128)}, u32[]{:S(2)}) copy-start(s32[32]{0:T(128)} %param.35) | copy-start | bytes 388
  154.8 12.5 %copy-start.13 = (f32[512,4]{0,1:T(4,128)S(1)}, f32[512,4]{0,1:T(4,128)}, u32[]{:S(2)}) copy-start(f32[512,4]{0,1:T(4,128)} %get-tuple-element.245) | copy-start | bytes 24580
  154.9 36.7 %copy-start.12 = (f32[512,4]{0,1:T(4,128)S(1)}, f32[512,4]{0,1:T(4,128)}, u32[]{:S(2)}) copy-start(f32[512,4]{0,1:T(4,128)} %get-tuple-element.226) | copy-start | bytes 24580
  216.0 23.9 %copy-start.15 = (f32[32,4]{0,1:T(4,128)S(1)}, f32[32,4]{0,1:T(4,128)}, u32[]{:S(2)}) copy-start(f32[32,4]{0,1:T(4,128)} %get-tuple-element.224) | copy-start | bytes 1540
  242.1 98.4 %reduce-scatter.2.cloned.1.call-start = ((), (), s32[]{:S(2)}) async-start(), calls=%async_computation.5 | async-start | bytes 294912 | tf_op jit(solution)/shard_map/reduce_scatter | solution.py:240
  252.3 12.5 %copy-start.16 = (bf16[2048]{0:T(1024)(128)(2,1)S(1)}, bf16[2048]{0:T(1024)(128)(2,1)}, u32[]{:S(2)}) copy-start(bf16[2048]{0:T(1024)(128)(2,1)} %param.22) | copy-start | bytes 12292
  252.3 49.5 %copy-start.7 = (bf16[32,2048]{1,0:T(8,128)(2,1)S(1)}, bf16[32,2048]{1,0:T(8,128)(2,1)}, u32[]{:S(2)}) copy-start(bf16[32,2048]{1,0:T(8,128)(2,1)} %param.20) | copy-start | bytes 393220
  302.9 6.2 %copy-start.5 = (bf16[1024,2048]{1,0:T(8,128)(2,1)S(1)}, bf16[1024,2048]{1,0:T(8,128)(2,1)}, u32[]{:S(2)}) copy-start(bf16[1024,2048]{1,0:T(8,128)(2,1)} %param.27) | copy-start | bytes 12582916
Sparse Core Ops, SparseCore 0:
  31.3 26.0 all-gather.4
  135.2 74.2 all-gather.6
  242.2 59.5 all-reduce.1
  310.7 29.6 reduce-scatter.1
